TPU v7x, 128 devices: a whole 4x4x4 slice. The times are simulated.
128 devices in a mesh: row: 8 (over z_hi, y), col: 16 (over x, z_lo, core).
Axes of the slice: x: 4, y: 4, z: 4 (z_hi: 2, z_lo: 2; z = z_hi * 2 + z_lo), core: 2. Of those that a mesh axis runs over, the one named last changes fastest.
Arguments:
- vectors: bfloat16 [32, 524288], P(None, ('row', 'col')), may hold values from -6 to 6
- tile_values: bfloat16 [81920, 128, 128], P(('row', 'col')), may hold values from -0.0546875 to 0.0546875
- tile_rows: int32 [81920], P(('row', 'col')), may hold values from 0 to 511
- tile_cols: int32 [81920], P(('row', 'col')), may hold values from 0 to 255
- tile_count: int32 [128], P(('row', 'col')), may hold values from 160 to 640, as said below
Outputs:
- filtered: bfloat16 [32, 524288], P(None, ('row', 'col'))
Inputs may be any that keep to these rules, and one draw needn't show every extreme that they name: `tile_count`: every device has at least a quarter of its slots live and some device has all 640 live.
All inputs are finite; a program needn't handle non-finite values.
Results may differ from a plain program's by a relative error of at most 0.014.
Values may be sent and summed in bfloat16 or wider, within the bound.
A program may use at most 128 MiB of HBM per device.

v0:
```python
import jax
import jax.numpy as jnp
from jax import lax
from jax.sharding import PartitionSpec as P


def one_hot_table(indices, count, dtype):
    return (indices[:, None] == jnp.arange(count, dtype=jnp.int32)[None, :]).astype(dtype)


def block_sums(terms, indices, count):
    table = one_hot_table(indices, count, jnp.float32)
    return jnp.einsum("tb,tki->bki", table, terms, precision=lax.Precision.HIGHEST)


def shards(vectors, tile_values, tile_rows, tile_cols, tile_count):
    features = vectors.shape[0]
    own_vertices = vectors.shape[1]
    slot_total = tile_values.shape[0]
    row_gathered = lax.all_gather(vectors, "col", axis=1, tiled=True)
    col_gathered = lax.all_gather(vectors, "row", axis=1, tiled=True)
    row_blocks = row_gathered.shape[1] // 128
    col_blocks = col_gathered.shape[1] // 128
    x_row = row_gathered.reshape(features, row_blocks, 128)
    x_col = col_gathered.reshape(features, col_blocks, 128)
    live_count = tile_count[0]
    alive = (jnp.arange(slot_total, dtype=jnp.int32) < live_count).astype(jnp.float32)
    picked_col = jnp.einsum(
        "tb,kbj->ktj",
        one_hot_table(tile_cols, col_blocks, jnp.bfloat16),
        x_col,
        preferred_element_type=jnp.float32,
    ).astype(jnp.bfloat16)
    picked_row = jnp.einsum(
        "tb,kbi->kti",
        one_hot_table(tile_rows, row_blocks, jnp.bfloat16),
        x_row,
        preferred_element_type=jnp.float32,
    ).astype(jnp.bfloat16)
    to_rows = jnp.einsum(
        "ktj,tij->tki", picked_col, tile_values, preferred_element_type=jnp.float32
    )
    to_cols = jnp.einsum(
        "kti,tij->tkj", picked_row, tile_values, preferred_element_type=jnp.float32
    )
    to_rows, to_cols = (to_rows * alive[:, None, None], to_cols * alive[:, None, None])
    col_sums = block_sums(to_cols, tile_cols, col_blocks)
    row_sums_all = block_sums(to_rows, tile_rows, row_blocks)
    mine_rows = lax.psum_scatter(
        row_sums_all.astype(jnp.bfloat16), "col", scatter_dimension=0, tiled=True
    ).astype(jnp.float32)
    mine_cols = lax.psum_scatter(
        col_sums.astype(jnp.bfloat16), "row", scatter_dimension=0, tiled=True
    ).astype(jnp.float32)
    combined = mine_rows + mine_cols
    return combined.transpose(1, 0, 2).reshape(features, own_vertices).astype(jnp.bfloat16)


def solution(mesh):
    in_specs = (
        P(None, ("row", "col")),
        P(("row", "col"), None, None),
        P(("row", "col")),
        P(("row", "col")),
        P(("row", "col")),
    )
    out_specs = P(None, ("row", "col"))
    return jax.shard_map(shards, mesh=mesh, in_specs=in_specs, out_specs=out_specs, check_vma=False)
```

profile of v0, /device:TPU:0, one launch (start us, length us, event | category | flops | bytes accessed | tf_op | source)
XLA Modules:
  0.0 266.3 jit_solution(13540595652899564749)
XLA Ops:
  6.5 0.0 all-gather.3.cloned.1.call-start
  6.5 0.7 all-gather.3.cloned.1.call-update
  7.3 0.0 all-gather.5.cloned.1.call-start
  7.3 0.7 all-gather.5.cloned.1.call-update
  8.0 0.0 reduce-scatter.3.cloned.1.call-start
  8.7 58.6 %all-gather.3.cloned.1.call-done = bf16[32,32768]{1,0:T(8,128)(2,1)} async-done(((bf16[32,4096]{1,0:T(8,128)(2,1)}), bf16[32,32768]{1,0:T(8,128)(2,1)}) %all-gather.3.cloned.1.call-update) | async-done | bytes 2097168 | tf_op jit(solution)/shard_map/all_gather | solution.py:21
  67.3 2.1 copy.10
  69.4 4.6 %fusion.20 = bf16[640,32,128]{2,0,1:T(8,128)(2,1)} fusion(bf16[32,256,128]{2,1,0:T(8,128)(2,1)S(1)} %bitcast.29, s32[640]{0:T(1024)} %param.8), kind=kOutput, calls=%fused_computation.21 | convolution fusion | flops 1342341120 | bytes 7342592 | tf_op jit(solution)/shard_map/tb,kbj->ktj/dot_general | solution.py:28
  74.0 0.0 copy-start.1
  74.0 20.2 %fusion.3 = f32[640,32,128]{2,1,0:T(8,128)} fusion(bf16[640,128,128]{2,1,0:T(8,128)(2,1)} %param.6, bf16[640,32,128]{2,0,1:T(8,128)(2,1)} %fusion.20), kind=kOutput, calls=%fused_computation.7 | convolution fusion | flops 671088640 | bytes 36700160 | tf_op jit(solution)/shard_map/ktj,tij->tki/dot_general | solution.py:40
  94.2 0.0 copy-done.1
  94.2 17.8 %fusion.10 = bf16[512,32,128]{2,0,1:T(8,128)(2,1)} fusion(f32[640,32,128]{2,1,0:T(8,128)} %fusion.3, f32[640]{0:T(1024)S(1)} %fusion.24, s32[640]{0:T(1024)S(1)} %copy-done.1), kind=kOutput, calls=%fused_computation.12 | convolution fusion | flops 16111173632 | bytes 14685184 | tf_op jit(solution)/shard_map/tb,tki->bki/dot_general | solution.py:13
  111.9 0.0 reduce-scatter.3.cloned.1.call-update
  112.0 0.0 reduce-scatter.5.cloned.1.call-start
  112.0 0.0 all-gather.5.cloned.1.call-done
  112.0 3.2 %copy.11 = bf16[4,8,512,128]{3,2,1,0:T(8,128)(2,1)S(1)} copy(bf16[4,8,512,128]{3,1,2,0:T(8,128)(2,1)} %bitcast.30) | data formatting | bytes 8388608
  115.2 4.9 %fusion.13 = bf16[640,32,128]{2,0,1:T(8,128)(2,1)} fusion(bf16[32,512,128]{2,1,0:T(8,128)(2,1)S(1)} %bitcast.31, s32[640]{0:T(1024)S(1)} %copy-done.1), kind=kOutput, calls=%fused_computation.16 | convolution fusion | flops 2684682240 | bytes 9439744 | tf_op jit(solution)/shard_map/tb,kbi->kti/dot_general | solution.py:34
  120.2 0.0 copy-start
  120.2 17.0 %fusion.6 = f32[640,32,128]{2,1,0:T(8,128)S(1)} fusion(bf16[640,128,128]{2,1,0:T(8,128)(2,1)} %param.6, bf16[640,32,128]{2,0,1:T(8,128)(2,1)} %fusion.13), kind=kOutput, calls=%fused_computation.9 | convolution fusion | flops 671088640 | bytes 36700160 | tf_op jit(solution)/shard_map/kti,tij->tkj/dot_general | solution.py:43
  137.1 0.0 copy-done
  137.1 16.5 %fusion.11 = bf16[256,32,128]{2,0,1:T(8,128)(2,1)} fusion(f32[640,32,128]{2,1,0:T(8,128)S(1)} %fusion.6, f32[640]{0:T(1024)S(1)} %fusion.24, s32[640]{0:T(1024)S(1)} %copy-done), kind=kOutput, calls=%fused_computation.13 | convolution fusion | flops 8056897536 | bytes 12588032 | tf_op jit(solution)/shard_map/tb,tki->bki/dot_general | solution.py:13
  153.7 0.0 reduce-scatter.5.cloned.1.call-update
  153.7 25.0 %reduce-scatter.3.cloned.1.call-done = bf16[32,32,128]{2,0,1:T(8,128)(2,1)} async-done(((bf16[512,32,128]{2,0,1:T(8,128)(2,1)}), bf16[32,32,128]{2,0,1:T(8,128)(2,1)}) %reduce-scatter.3.cloned.1.call-update) | async-done | bytes 262160 | tf_op jit(solution)/shard_map/reduce_scatter | solution.py:49
  178.7 79.1 %reduce-scatter.5.cloned.1.call-done = bf16[32,32,128]{2,0,1:T(8,128)(2,1)} async-done(((bf16[256,32,128]{2,0,1:T(8,128)(2,1)}), bf16[32,32,128]{2,0,1:T(8,128)(2,1)}) %reduce-scatter.5.cloned.1.call-update) | async-done | bytes 262160 | tf_op jit(solution)/shard_map/reduce_scatter | solution.py:52
  257.8 1.1 add_convert_fusion
  258.9 0.8 copy.30
  (1 shorter events, 0.0 us)
Async XLA Ops:
  6.5 60.8 %all-gather.3.cloned.1.call-start = ((), (), s32[]{:S(2)}) async-start(), calls=%async_computation.2 | async-start | bytes 2359296 | tf_op jit(solution)/shard_map/all_gather | solution.py:21
  7.3 104.8 %all-gather.5.cloned.1.call-start = ((), (), s32[]{:S(2)}) async-start(), calls=%async_computation.4 | async-start | bytes 4456448 | tf_op jit(solution)/shard_map/all_gather | solution.py:20
  8.0 170.7 %reduce-scatter.3.cloned.1.call-start = ((), (), s32[]{:S(2)}) async-start(), calls=%async_computation.3 | async-start | bytes 4456448 | tf_op jit(solution)/shard_map/reduce_scatter | solution.py:49
  74.0 20.2 %copy-start.1 = (s32[640]{0:T(1024)S(1)}, s32[640]{0:T(1024)}, u32[]{:S(2)}) copy-start(s32[640]{0:T(1024)} %param.7) | copy-start | bytes 7684
  112.0 145.9 %reduce-scatter.5.cloned.1.call-start = ((), (), s32[]{:S(2)}) async-start(), calls=%async_computation.5 | async-start | bytes 2359296 | tf_op jit(solution)/shard_map/reduce_scatter | solution.py:52
  120.2 17.0 %copy-start = (s32[640]{0:T(1024)S(1)}, s32[640]{0:T(1024)}, u32[]{:S(2)}) copy-start(s32[640]{0:T(1024)} %param.8) | copy-start | bytes 7684
Sparse Core Ops, SparseCore 0:
  9.7 57.5 all-gather.2
  69.0 35.7 all-gather.4
  112.1 66.5 reduce-scatter.2
  182.3 75.4 reduce-scatter.4
where the time goes:
time: 267 us; the launch traced here: 266 us
  waiting for transfers between devices  164 us (61%)
  matrix products  81 us (30%)
  between operations  13.8 us (5%)
  local copies, waits for them, and re-layouts  6.07 us (2%)
    reduce_scatter x1, waiting for transfers between devices, shards(): lax.psum_scatter(col_sums.astype(jnp.bfloat16), 'row', scatter_dimension=...  79.1 us
    all_gather x1, waiting for transfers between devices, shards(): col_gathered = lax.all_gather(vectors, 'row', axis=1, tiled=True)  58.6 us
    dot_general x2, matrix products, block_sums(): jnp.einsum('tb,tki->bki', table, terms, precision=lax.Precision.HIGHEST)  34.3 us
    reduce_scatter x1, waiting for transfers between devices, shards(): lax.psum_scatter(row_sums_all.astype(jnp.bfloat16), 'col', scatter_dimens...  25 us
    dot_general x1, matrix products, shards(): jnp.einsum('ktj,tij->tki', picked_col, tile_values, preferred_element_typ...  20.2 us
    dot_general x1, matrix products, shards(): jnp.einsum('kti,tij->tkj', picked_row, tile_values, preferred_element_typ...  17 us
    unnamed x7, local copies, waits for them, and re-layouts  6.07 us
  transfers between devices with their start and end apart: 4, of which 3 were waited for; matrix products, arithmetic and copies ran while one was open for 32% of the time, Pallas kernels for 0%

commit v1 on v0

--- a/solution.py
+++ b/solution.py
@@ -18,7 +18,15 @@
     own_vertices = vectors.shape[1]
     slot_total = tile_values.shape[0]
     row_gathered = lax.all_gather(vectors, "col", axis=1, tiled=True)
-    col_gathered = lax.all_gather(vectors, "row", axis=1, tiled=True)
+    col_gathered = jnp.concatenate(
+        lax.all_to_all(
+            jnp.stack([vectors] * lax.axis_size("row")),
+            concat_axis=0,
+            split_axis=0,
+            axis_name="row",
+        ),
+        1,
+    )
     row_blocks = row_gathered.shape[1] // 128
     col_blocks = col_gathered.shape[1] // 128
     x_row = row_gathered.reshape(features, row_blocks, 128)

time: 267 us -> 253 us (0.948)
  waiting for transfers between devices: 164 us -> 136 us
  starting transfers between devices: 0.12 us -> 7.98 us
  local copies, waits for them, and re-layouts: 6.07 us -> 11.9 us
    all_gather x1 -> x0, waiting for transfers between devices: 58.6 us -> none  [shards(): col_gathered = lax.all_gather(vectors, 'row', axis=1, tiled=True)]
    all_to_all x0 -> x1, waiting for transfers between devices: none -> 29.9 us  [shards(): lax.all_to_all(jnp.stack([vectors] * lax.axis_size('row')), concat_axis=0...]
    all_to_all x0 -> x1, starting transfers between devices: none -> 7.89 us  [shards(): lax.all_to_all(jnp.stack([vectors] * lax.axis_size('row')), concat_axis=0...]
    another operation x0 -> x2, local copies, waits for them, and re-layouts: none -> 5.43 us  [the longest x1 2.89 us: shards(): x_col = col_gathered.reshape(features, col_blocks, 128)]
    unnamed x7 -> x6, local copies, waits for them, and re-layouts: 6.07 us -> 3.99 us
  transfers between devices with their start and end apart: 4 -> 4, of which waited for: 3 -> 3; matrix products, arithmetic and copies ran while one was open for 32% -> 37% of each run, Pallas kernels for 0% -> 0%
where the time goes in v1:
time: 253 us
  waiting for transfers between devices  136 us (54%)
  matrix products  82.2 us (32%)
  between operations  13.8 us (5%)
  local copies, waits for them, and re-layouts  11.9 us (5%)
  starting transfers between devices  7.98 us (3%)
    reduce_scatter x1, waiting for transfers between devices, shards(): lax.psum_scatter(col_sums.astype(jnp.bfloat16), 'row', scatter_dimension=...  79.2 us
    dot_general x2, matrix products, block_sums(): jnp.einsum('tb,tki->bki', table, terms, precision=lax.Precision.HIGHEST)  34.1 us
    all_to_all x1, waiting for transfers between devices, shards(): lax.all_to_all(jnp.stack([vectors] * lax.axis_size('row')), concat_axis=0...  29.9 us
    reduce_scatter x1, waiting for transfers between devices, shards(): lax.psum_scatter(row_sums_all.astype(jnp.bfloat16), 'col', scatter_dimens...  25.7 us
    dot_general x1, matrix products, shards(): jnp.einsum('ktj,tij->tki', picked_col, tile_values, preferred_element_typ...  20.9 us
    dot_general x1, matrix products, shards(): jnp.einsum('kti,tij->tkj', picked_row, tile_values, preferred_element_typ...  18.3 us
    all_to_all x1, starting transfers between devices, shards(): lax.all_to_all(jnp.stack([vectors] * lax.axis_size('row')), concat_axis=0...  7.89 us
  transfers between devices with their start and end apart: 4, of which 3 were waited for; matrix products, arithmetic and copies ran while one was open for 37% of the time, Pallas kernels for 0%

profile of v1, /device:TPU:0, one launch (start us, length us, event | category | flops | bytes accessed | tf_op | source)
XLA Modules:
  0.0 252.6 jit_solution(12541569753730291486)
XLA Ops:
  6.5 0.0 all-gather.2.cloned.1.call-start
  6.5 0.7 all-gather.2.cloned.1.call-update
  7.3 2.5 %stack.2 = bf16[8,32,4096]{2,1,0:T(8,128)(2,1)} broadcast(bf16[32,4096]{1,0:T(8,128)(2,1)} %param.5), dimensions={1,2} | broadcast | bytes 2359296 | tf_op jit(solution)/shard_map/stack | solution.py:23
  9.8 7.9 %all-to-all-start = ((bf16[8,32,4096]{2,1,0:T(8,128)(2,1)}), bf16[8,32,4096]{2,1,0:T(8,128)(2,1)S(1)}, u32[]{:S(2)}, u32[]{:S(2)}) async-start(bf16[8,32,4096]{2,1,0:T(8,128)(2,1)} %stack.2), calls=%async_computation | async-start | bytes 4194304 | tf_op jit(solution)/shard_map/all_to_all | solution.py:22
  17.7 0.0 copy-start
  17.7 0.0 reduce-scatter.3.cloned.1.call-start
  18.4 29.9 %all-to-all-done = bf16[8,32,4096]{2,1,0:T(8,128)(2,1)S(1)} async-done(((bf16[8,32,4096]{2,1,0:T(8,128)(2,1)}), bf16[8,32,4096]{2,1,0:T(8,128)(2,1)S(1)}, u32[]{:S(2)}, u32[]{:S(2)}) %all-to-all-start) | async-done | bytes 2097184 | tf_op jit(solution)/shard_map/all_to_all | solution.py:22
  48.3 2.5 copy.6
  50.8 2.9 %reshape_reshape.3 = bf16[32,256,128]{2,1,0:T(8,128)(2,1)S(1)} reshape(bf16[32,8,4096]{2,1,0:T(8,128)(2,1)} %copy.6) | data formatting | bytes 4194304 | tf_op jit(solution)/shard_map/reshape;reshape | solution.py:33
  53.7 0.0 copy-done
  53.7 3.9 %convert_bitcast_fusion.1 = bf16[32,640,128]{2,1,0:T(8,128)(2,1)} fusion(bf16[32,256,128]{2,1,0:T(8,128)(2,1)S(1)} %reshape_reshape.3, s32[640]{0:T(1024)S(1)} %copy-done), kind=kOutput, calls=%fused_computation.11 | convolution fusion | flops 1344962560 | bytes 7342592 | tf_op jit(solution)/shard_map/tb,kbj->ktj/dot_general | solution.py:36
  57.7 0.0 copy-start.1
  57.7 20.9 %broadcast_multiply_fusion.1 = f32[640,32,128]{2,1,0:T(8,128)} fusion(f32[640]{0:T(1024)S(1)} %fusion.28, bf16[640,128,128]{2,1,0:T(8,128)(2,1)} %param.6, bf16[32,640,128]{2,1,0:T(8,128)(2,1)} %convert_bitcast_fusion.1), kind=kOutput, calls=%fused_computation.10 | convolution fusion | flops 673710080 | bytes 36702720 | tf_op jit(solution)/shard_map/ktj,tij->tki/dot_general | solution.py:48
  78.6 0.0 copy-done.1
  78.6 17.9 %fusion.12 = bf16[512,32,128]{2,0,1:T(8,128)(2,1)} fusion(f32[640,32,128]{2,1,0:T(8,128)} %broadcast_multiply_fusion.1, s32[640]{0:T(1024)S(1)} %copy-done.1), kind=kOutput, calls=%fused_computation.12 | convolution fusion | flops 16108552192 | bytes 14682624 | tf_op jit(solution)/shard_map/tb,tki->bki/dot_general | solution.py:13
  96.5 0.0 reduce-scatter.3.cloned.1.call-update
  96.5 0.0 reduce-scatter.5.cloned.1.call-start
  96.5 0.0 all-gather.2.cloned.1.call-done
  96.6 3.2 %copy.17 = bf16[4,8,512,128]{3,2,1,0:T(8,128)(2,1)S(1)} copy(bf16[4,8,512,128]{3,1,2,0:T(8,128)(2,1)} %bitcast.29) | data formatting | bytes 8388608
  99.8 5.0 %convert_bitcast_fusion = bf16[32,640,128]{2,1,0:T(8,128)(2,1)} fusion(bf16[32,512,128]{2,1,0:T(8,128)(2,1)S(1)} %bitcast.30, s32[640]{0:T(1024)S(1)} %copy-done.1), kind=kOutput, calls=%fused_computation.8 | convolution fusion | flops 2687303680 | bytes 9439744 | tf_op jit(solution)/shard_map/tb,kbi->kti/dot_general | solution.py:42
  104.8 18.3 %broadcast_multiply_fusion = f32[640,32,128]{2,1,0:T(8,128)S(1)} fusion(f32[640]{0:T(1024)S(1)} %fusion.28, bf16[640,128,128]{2,1,0:T(8,128)(2,1)} %param.6, bf16[32,640,128]{2,1,0:T(8,128)(2,1)} %convert_bitcast_fusion), kind=kOutput, calls=%fused_computation.9 | convolution fusion | flops 673710080 | bytes 36702720 | tf_op jit(solution)/shard_map/kti,tij->tkj/dot_general | solution.py:51
  123.1 16.2 %fusion.15 = bf16[256,32,128]{2,0,1:T(8,128)(2,1)} fusion(f32[640,32,128]{2,1,0:T(8,128)S(1)} %broadcast_multiply_fusion, s32[640]{0:T(1024)S(1)} %copy-done), kind=kOutput, calls=%fused_computation.13 | convolution fusion | flops 8054276096 | bytes 12585472 | tf_op jit(solution)/shard_map/tb,tki->bki/dot_general | solution.py:13
  139.3 0.0 reduce-scatter.5.cloned.1.call-update
  139.3 25.7 %reduce-scatter.3.cloned.1.call-done = bf16[32,32,128]{2,0,1:T(8,128)(2,1)} async-done(((bf16[512,32,128]{2,0,1:T(8,128)(2,1)}), bf16[32,32,128]{2,0,1:T(8,128)(2,1)}) %reduce-scatter.3.cloned.1.call-update) | async-done | bytes 262160 | tf_op jit(solution)/shard_map/reduce_scatter | solution.py:57
  165.0 79.2 %reduce-scatter.5.cloned.1.call-done = bf16[32,32,128]{2,0,1:T(8,128)(2,1)} async-done(((bf16[256,32,128]{2,0,1:T(8,128)(2,1)}), bf16[32,32,128]{2,0,1:T(8,128)(2,1)}) %reduce-scatter.5.cloned.1.call-update) | async-done | bytes 262160 | tf_op jit(solution)/shard_map/reduce_scatter | solution.py:60
  244.2 1.1 add_convert_fusion
  245.3 0.8 copy.36
  (1 shorter events, 0.0 us)
Async XLA Ops:
  6.5 90.0 %all-gather.2.cloned.1.call-start = ((), (), s32[]{:S(2)}) async-start(), calls=%async_computation.4 | async-start | bytes 4456448 | tf_op jit(solution)/shard_map/all_gather | solution.py:20
  9.8 38.5 %all-to-all-start = ((bf16[8,32,4096]{2,1,0:T(8,128)(2,1)}), bf16[8,32,4096]{2,1,0:T(8,128)(2,1)S(1)}, u32[]{:S(2)}, u32[]{:S(2)}) async-start(bf16[8,32,4096]{2,1,0:T(8,128)(2,1)} %stack.2), calls=%async_computation | async-start | bytes 4194304 | tf_op jit(solution)/shard_map/all_to_all | solution.py:22
  17.7 36.0 %copy-start = (s32[640]{0:T(1024)S(1)}, s32[640]{0:T(1024)}, u32[]{:S(2)}) copy-start(s32[640]{0:T(1024)} %param.8) | copy-start | bytes 7684
  17.7 147.3 %reduce-scatter.3.cloned.1.call-start = ((), (), s32[]{:S(2)}) async-start(), calls=%async_computation.3 | async-start | bytes 4456448 | tf_op jit(solution)/shard_map/reduce_scatter | solution.py:57
  57.7 20.9 %copy-start.1 = (s32[640]{0:T(1024)S(1)}, s32[640]{0:T(1024)}, u32[]{:S(2)}) copy-start(s32[640]{0:T(1024)} %param.7) | copy-start | bytes 7684
  96.5 147.7 %reduce-scatter.5.cloned.1.call-start = ((), (), s32[]{:S(2)}) async-start(), calls=%async_computation.5 | async-start | bytes 2359296 | tf_op jit(solution)/shard_map/reduce_scatter | solution.py:60
Sparse Core Ops, SparseCore 0:
  9.0 57.9 all-gather.1
  96.6 68.3 reduce-scatter.2
  168.8 75.3 reduce-scatter.4
